TPU v7x, 32 devices: a whole 2x2x4 slice. The times are simulated.
32 devices in a mesh: expert: 8 (over z, y), ctx: 4 (over x, core).
Axes of the slice: x: 2, y: 2, z: 4, core: 2. Of those that a mesh axis runs over, the one named last changes fastest.
Arguments:
- resid: bfloat16 [4096, 2048], P(('expert', 'ctx')), may hold values from -30 to 30
- queries: bfloat16 [4096, 2048], P(('expert', 'ctx')), may hold values from -8 to 8
- keys: bfloat16 [4096, 2048], P(('expert', 'ctx')), may hold values from -8 to 8
- values: bfloat16 [4096, 2048], P(('expert', 'ctx')), may hold values from -6 to 6
- mod_scale: float32 [8, 2048], P('expert'), may hold values from -0.5 to 0.5
- mod_shift: float32 [8, 2048], P('expert'), may hold values from -3 to 3
- mod_gate: float32 [8, 2048], P('expert'), may hold values from 0.5 to 1.5
- router: bfloat16 [2048, 8], replicated, may hold values from -0.125 to 0.125
- w_in: bfloat16 [8, 2048, 1024], P('expert', None, 'ctx'), may hold values from -0.125 to 0.125
- w_out: bfloat16 [8, 1024, 2048], P('expert', 'ctx'), may hold values from -0.1875 to 0.1875
- expert_ids: int32 [4096, 2], P(('expert', 'ctx')), may hold values from 0 to 7, all different within a row; in each aligned block of 128 rows (0 to 127, 128 to 255, ...) at most 40 rows name the same one
- grad_out: bfloat16 [4096, 2048], P(('expert', 'ctx')), may hold values from -1.5 to 1.5
Outputs:
- mixed_out: bfloat16 [4096, 2048], P(('expert', 'ctx'))
- resid_grad: bfloat16 [4096, 2048], P(('expert', 'ctx'))
- grad_queries: bfloat16 [4096, 2048], P(('expert', 'ctx'))
- grad_keys: bfloat16 [4096, 2048], P(('expert', 'ctx'))
- grad_values: bfloat16 [4096, 2048], P(('expert', 'ctx'))
- grad_w_in: bfloat16 [8, 2048, 1024], P('expert', None, 'ctx')
- grad_w_out: bfloat16 [8, 1024, 2048], P('expert', 'ctx')
- grad_router: float32 [2048, 8], replicated
Inputs may be any that keep to these rules, and one draw needn't show every extreme that they name: `expert_ids`: each token names two different experts. Within one aligned block of 128 tokens no expert is named by more than 40 tokens, and some block reaches 40.
All inputs are finite; a program needn't handle non-finite values.
Results may differ from a plain program's by a relative error of at most 0.013.
The roundings to bfloat16 on the way count: a program that leaves them out, or rounds other values in their place, can miss the bound.
Values may be sent and summed in bfloat16 or wider, within the bound.
A program may use at most 128 MiB of HBM per device.

v0:
```python
import math
import jax
import jax.numpy as jnp
from jax import lax
from jax.sharding import PartitionSpec as P

HEADS = 16
NORM_EPSILON = 1e-06


def rounded(value):
    return lax.optimization_barrier(value.astype(jnp.bfloat16)).astype(jnp.float32)


def contract_rows(left_side, right_side):
    return lax.dot_general(
        left_side, right_side, (((0,), (0,)), ((), ())), preferred_element_type=jnp.float32
    )


def contract_cols(left_side, right_side):
    return lax.dot_general(
        left_side, right_side, (((1,), (1,)), ((), ())), preferred_element_type=jnp.float32
    )


def local(
    resid,
    queries,
    keys,
    values,
    mod_scale,
    mod_shift,
    mod_gate,
    router,
    w_in,
    w_out,
    expert_ids,
    grad_out,
):
    tok_rows, width = resid.shape
    head_size = width // HEADS
    score_scale = 1.0 / math.sqrt(head_size)
    experts = router.shape[1]
    capacity = 5 * tok_rows // (2 * experts)
    groups = lax.axis_size("ctx")
    block_units = w_in.shape[2]
    clip_keys, clip_values = (
        lax.all_gather(keys, "ctx", axis=0, tiled=True),
        lax.all_gather(values, "ctx", axis=0, tiled=True),
    )
    clip_len = clip_keys.shape[0]
    query_heads = queries.reshape(tok_rows, HEADS, head_size)
    key_heads = clip_keys.reshape(clip_len, HEADS, head_size)
    value_heads = clip_values.reshape(clip_len, HEADS, head_size)
    scores = (
        jnp.einsum("qhd,khd->hqk", query_heads, key_heads, preferred_element_type=jnp.float32)
        * score_scale
    )
    row_top = jnp.max(scores, axis=-1)
    exp_scores = jnp.exp(scores - row_top[..., None])
    row_total = jnp.sum(exp_scores, axis=-1)
    mixed_values = jnp.einsum(
        "hqk,khd->qhd",
        exp_scores.astype(jnp.bfloat16),
        value_heads,
        preferred_element_type=jnp.float32,
    )
    attn_heads = (mixed_values / row_total.T[:, :, None]).astype(jnp.bfloat16)
    log_total = row_top + jnp.log(row_total)
    hidden_sum = resid.astype(jnp.float32) + attn_heads.reshape(tok_rows, width).astype(jnp.float32)
    inv_rms = lax.rsqrt(jnp.mean(hidden_sum * hidden_sum, axis=-1, keepdims=True) + NORM_EPSILON)
    normed = hidden_sum * inv_rms
    lift_gain = 1.0 + mod_scale
    normed_mod = (normed * lift_gain + mod_shift).astype(jnp.bfloat16)
    logits = jnp.dot(normed_mod, router, preferred_element_type=jnp.float32)
    expert_range = jnp.arange(experts, dtype=jnp.int32)
    first_hot = (expert_ids[:, 0:1] == expert_range[None, :]).astype(jnp.float32)
    second_hot = (expert_ids[:, 1:2] == expert_range[None, :]).astype(jnp.float32)
    margin = jnp.sum(logits * first_hot, axis=-1) - jnp.sum(logits * second_hot, axis=-1)
    gate_one = jax.nn.sigmoid(margin)
    gate_two = 1.0 - gate_one
    both_hot = first_hot + second_hot
    earlier = jnp.cumsum(both_hot, axis=0) - both_hot
    place_one = expert_ids[:, 0] * capacity + jnp.sum(earlier * first_hot, axis=-1).astype(
        jnp.int32
    )
    place_two = expert_ids[:, 1] * capacity + jnp.sum(earlier * second_hot, axis=-1).astype(
        jnp.int32
    )
    slot_range = jnp.arange(experts * capacity, dtype=jnp.int32)
    pick_one = (place_one[:, None] == slot_range[None, :]).astype(jnp.bfloat16)
    pick_two = (place_two[:, None] == slot_range[None, :]).astype(jnp.bfloat16)
    sent_rows = (
        contract_rows(pick_one + pick_two, normed_mod)
        .astype(jnp.bfloat16)
        .reshape(experts, capacity, width)
    )
    full_in, full_out = (
        lax.all_gather(w_in, "ctx", axis=2, tiled=True),
        lax.all_gather(w_out, "ctx", axis=1, tiled=True),
    )
    full_in = full_in[0]
    full_out = full_out[0]
    arrived = lax.all_to_all(sent_rows, "expert", split_axis=0, concat_axis=0, tiled=True)
    item_count = arrived.shape[1]
    flat_rows = arrived.reshape(-1, width)
    pre_act = jnp.dot(flat_rows, full_in, preferred_element_type=jnp.float32)
    activated = jax.nn.gelu(pre_act).astype(jnp.bfloat16)
    block_sum = jnp.zeros((flat_rows.shape[0], width), jnp.float32)
    for expert_block_index in range(groups):
        expert_low_col = expert_block_index * block_units
        block_sum = block_sum + rounded(
            jnp.dot(
                activated[:, expert_low_col : expert_low_col + block_units],
                full_out[expert_low_col : expert_low_col + block_units],
                preferred_element_type=jnp.float32,
            )
        )
    returned = lax.all_to_all(
        block_sum.astype(jnp.bfloat16).reshape(experts, item_count, width),
        "expert",
        split_axis=0,
        concat_axis=0,
        tiled=True,
    )
    kept_pre = pre_act.reshape(experts, item_count, -1)
    kept_act = activated.reshape(experts, item_count, -1)
    home_flat = returned.reshape(experts * capacity, width)
    result_one = jnp.dot(pick_one, home_flat, preferred_element_type=jnp.float32)
    result_two = jnp.dot(pick_two, home_flat, preferred_element_type=jnp.float32)
    branch = gate_one[:, None] * result_one + gate_two[:, None] * result_two
    mixed_out = (hidden_sum + mod_gate * branch).astype(jnp.bfloat16)
    grad_float = grad_out.astype(jnp.float32)
    branch_grad = mod_gate * grad_float
    grad_one = (gate_one[:, None] * branch_grad).astype(jnp.bfloat16)
    grad_two = (gate_two[:, None] * branch_grad).astype(jnp.bfloat16)
    gate_tilt = (
        (jnp.sum(branch_grad * result_one, axis=-1) - jnp.sum(branch_grad * result_two, axis=-1))
        * gate_one
        * gate_two
    )
    logit_grad = (gate_tilt[:, None] * (first_hot - second_hot)).astype(jnp.bfloat16)
    grad_router = lax.psum(contract_rows(normed_mod, logit_grad), ("expert", "ctx"))
    back_router = contract_cols(logit_grad, router)
    sent_grads = (contract_rows(pick_one, grad_one) + contract_rows(pick_two, grad_two)).astype(
        jnp.bfloat16
    )
    sent_grads = sent_grads.reshape(experts, capacity, width)
    arrived_grads = lax.all_to_all(sent_grads, "expert", split_axis=0, concat_axis=0, tiled=True)
    rows_flat = arrived.reshape(-1, width)
    pre_flat = kept_pre.reshape(-1, kept_pre.shape[2])
    act_flat = kept_act.reshape(-1, kept_act.shape[2])
    gelu_pull = jax.vjp(jax.nn.gelu, pre_flat)[1]
    grad_flat = arrived_grads.reshape(-1, width)
    pre_grad = gelu_pull(contract_cols(grad_flat, full_out))[0].astype(jnp.bfloat16)
    block_sum = jnp.zeros((grad_flat.shape[0], width), jnp.float32)
    for block_index in range(groups):
        low_col = block_index * block_units
        block_sum = block_sum + rounded(
            contract_cols(
                pre_grad[:, low_col : low_col + block_units],
                full_in[:, low_col : low_col + block_units],
            )
        )
    back_rows = lax.all_to_all(
        block_sum.astype(jnp.bfloat16).reshape(experts, capacity, width),
        "expert",
        split_axis=0,
        concat_axis=0,
        tiled=True,
    )
    weight_sums = lax.psum_scatter(
        jnp.concatenate(
            [contract_rows(pre_grad, rows_flat), contract_rows(act_flat, grad_flat)], axis=1
        ).astype(jnp.bfloat16),
        "ctx",
        scatter_dimension=0,
        tiled=True,
    ).astype(jnp.float32)
    grad_w_in = weight_sums[:, :width].T.astype(jnp.bfloat16)[None]
    grad_w_out = weight_sums[:, width:].astype(jnp.bfloat16)[None]
    back_flat = back_rows.reshape(experts * capacity, width)
    input_grad = (
        jnp.dot(pick_one, back_flat, preferred_element_type=jnp.float32)
        + jnp.dot(pick_two, back_flat, preferred_element_type=jnp.float32)
        + back_router
    )
    lifted = input_grad * lift_gain
    resid_grad = grad_float + inv_rms * (
        lifted - normed * jnp.mean(lifted * normed, axis=-1, keepdims=True)
    )
    resid_grad = resid_grad.astype(jnp.bfloat16)
    grad_heads = resid_grad.reshape(tok_rows, HEADS, head_size)
    prob = jnp.exp(scores - log_total[..., None])
    prob_low = prob.astype(jnp.bfloat16)
    value_pull = jnp.einsum(
        "qhd,khd->hqk", grad_heads, value_heads, preferred_element_type=jnp.float32
    )
    row_dot = jnp.einsum("qhd,qhd->hq", grad_heads, attn_heads, preferred_element_type=jnp.float32)
    score_grad = (prob * (value_pull - row_dot[..., None])).astype(jnp.bfloat16)
    grad_queries = (
        (
            jnp.einsum("hqk,khd->qhd", score_grad, key_heads, preferred_element_type=jnp.float32)
            * score_scale
        )
        .astype(jnp.bfloat16)
        .reshape(tok_rows, width)
    )
    row_count = lax.axis_size("ctx") * tok_rows
    key_term = rounded(
        jnp.einsum("hqk,qhd->khd", score_grad, query_heads, preferred_element_type=jnp.float32)
        * score_scale
    )
    value_term = rounded(
        jnp.einsum("hqk,qhd->khd", prob_low, grad_heads, preferred_element_type=jnp.float32)
    )
    key_sums = lax.psum_scatter(
        jnp.concatenate(
            [key_term.reshape(row_count, width), value_term.reshape(row_count, width)], axis=1
        ).astype(jnp.bfloat16),
        "ctx",
        scatter_dimension=0,
        tiled=True,
    ).astype(jnp.float32)
    grad_keys = key_sums[:, :width].astype(jnp.bfloat16)
    grad_values = key_sums[:, width:].astype(jnp.bfloat16)
    return (
        mixed_out,
        resid_grad,
        grad_queries,
        grad_keys,
        grad_values,
        grad_w_in,
        grad_w_out,
        grad_router,
    )


def solution(mesh):
    return jax.shard_map(
        local,
        mesh=mesh,
        in_specs=(
            P(("expert", "ctx"), None),
            P(("expert", "ctx"), None),
            P(("expert", "ctx"), None),
            P(("expert", "ctx"), None),
            P("expert", None),
            P("expert", None),
            P("expert", None),
            P(),
            P("expert", None, "ctx"),
            P("expert", "ctx", None),
            P(("expert", "ctx"), None),
            P(("expert", "ctx"), None),
        ),
        out_specs=(
            P(("expert", "ctx"), None),
            P(("expert", "ctx"), None),
            P(("expert", "ctx"), None),
            P(("expert", "ctx"), None),
            P(("expert", "ctx"), None),
            P("expert", None, "ctx"),
            P("expert", "ctx", None),
            P(),
        ),
        check_vma=False,
    )
```

profile of v0, /device:TPU:1, one launch (start us, length us, event | category | flops | bytes accessed | tf_op | source)
XLA Modules:
  0.0 538.3 jit_solution(17121193874179204365)
XLA Ops:
  8.0 2.0 copy.51
  11.7 22.9 %all-gather.7.cloned.1.call-done = bf16[512,2048]{1,0:T(8,128)(2,1)} async-done(((bf16[128,2048]{1,0:T(8,128)(2,1)}), bf16[512,2048]{1,0:T(8,128)(2,1)}) %all-gather.7.cloned.1.call-update) | async-done | bytes 2097168 | tf_op jit(solution)/shard_map/all_gather | solution.py:50
  34.6 2.9 copy.54
  37.5 22.1 %all-gather.5.cloned.1.call-done = bf16[512,2048]{0,1:T(8,128)(2,1)} async-done(((bf16[128,2048]{0,1:T(8,128)(2,1)}), bf16[512,2048]{0,1:T(8,128)(2,1)}) %all-gather.5.cloned.1.call-update) | async-done | bytes 2097168 | tf_op jit(solution)/shard_map/all_gather | solution.py:49
  59.6 2.4 multiply_reduce_fusion
  68.5 35.7 %all_to_all.20 = bf16[8,40,2048]{2,1,0:T(8,128)(2,1)} all-to-all(bf16[8,40,2048]{2,1,0:T(8,128)(2,1)S(1)} %bitcast.130), channel_id=1, replica_groups=mesh['expert'=8,'ctx'=4] {'expert'}, dimensions={0} | all-to-all | bytes 2621440 | tf_op jit(solution)/shard_map/all_to_all | solution.py:105
  104.3 6.1 %multiply_convert_fusion.2 = (bf16[320,1024]{1,0:T(8,128)(2,1)S(1)}, f32[320,1024]{1,0:T(8,128)}) fusion(bf16[320,2048]{1,0:T(8,128)(2,1)} %bitcast.140, bf16[1,2048,1024]{2,1,0:T(8,128)(2,1)} %all-gather.9.cloned.1.call-done), kind=kOutput, calls=%fused_computation.55 | convolution fusion | flops 1345126400 | bytes 7471104 | tf_op jit(solution)/shard_map/dot_general | solution.py:108
  110.4 21.7 %all-gather.11.cloned.1.call-done = bf16[1,1024,2048]{2,1,0:T(8,128)(2,1)} async-done(((bf16[1,256,2048]{2,1,0:T(8,128)(2,1)}), bf16[1,1024,2048]{2,1,0:T(8,128)(2,1)}) %all-gather.11.cloned.1.call-update) | async-done | bytes 4194320 | tf_op jit(solution)/shard_map/all_gather | solution.py:101
  132.1 1.9 convolution_convert_fusion.7
  134.0 1.7 convolution_convert_fusion.8
  137.9 35.8 %all_to_all.21 = bf16[8,40,2048]{2,1,0:T(8,128)(2,1)S(1)} all-to-all(bf16[8,40,2048]{2,1,0:T(8,128)(2,1)S(1)} %bitcast.132), channel_id=1, replica_groups=mesh['expert'=8,'ctx'=4] {'expert'}, dimensions={0} | all-to-all | bytes 2621440 | tf_op jit(solution)/shard_map/all_to_all | solution.py:120
  174.1 1.5 fusion.38
  177.0 34.8 %all_to_all.22 = bf16[8,40,2048]{2,1,0:T(8,128)(2,1)S(1)} all-to-all(bf16[8,40,2048]{2,1,0:T(8,128)(2,1)S(1)} %bitcast.129), channel_id=1, replica_groups=mesh['expert'=8,'ctx'=4] {'expert'}, dimensions={0} | all-to-all | bytes 2621440 | tf_op jit(solution)/shard_map/all_to_all | solution.py:150
  211.8 2.2 fusion.31
  216.7 2.0 add_convert_fusion
  218.7 4.1 all-to-all-start.3
  223.1 29.9 %all-to-all-done.3 = bf16[8,40,2048]{2,1,0:T(8,128)(2,1)S(1)} async-done(((bf16[8,40,2048]{2,1,0:T(8,128)(2,1)}), bf16[8,40,2048]{2,1,0:T(8,128)(2,1)S(1)}, u32[]{:S(2)}, u32[]{:S(2)}) %all-to-all-start.3) | async-done | bytes 1310752 | tf_op jit(solution)/shard_map/all_to_all | solution.py:166
  261.2 4.7 convert_bitcast_fusion
  267.3 2.2 fusion.17
  269.6 3.9 copy.62
  273.5 4.5 pad_maximum_fusion.1
  277.9 6.4 %copy.77 = bf16[512,4096]{1,0:T(8,128)(2,1)} copy(bf16[512,4096]{0,1:T(8,128)(2,1)} %pad_maximum_fusion.1) | data formatting | bytes 8388608
  284.4 6.1 %convolution_convert_fusion.1 = bf16[1024,2048]{1,0:T(8,128)(2,1)} fusion(bf16[320,1024]{1,0:T(8,128)(2,1)} %copy-done.22, bf16[320,2048]{1,0:T(8,128)(2,1)} %bitcast.141), kind=kOutput, calls=%fused_computation.9 | convolution fusion | flops 1344274432 | bytes 6160384 | tf_op jit(solution)/shard_map/dot_general | solution.py:16
  290.5 4.3 convolution_convert_fusion
  294.9 7.9 %pad_maximum_fusion = bf16[1024,4096]{1,0:T(8,128)(2,1)} fusion(bf16[1024,2048]{1,0:T(8,128)(2,1)} %convolution_convert_fusion, bf16[1024,2048]{1,0:T(8,128)(2,1)} %convolution_convert_fusion.1), kind=kLoop, calls=%fused_computation | loop fusion | flops 16777216 | bytes 16777216 | tf_op jit(solution)/shard_map/concatenate | solution.py:174
  304.8 2.3 fusion.32
  308.2 20.3 %reduce-scatter.7.cloned.1.call-done = bf16[128,4096]{1,0:T(8,128)(2,1)} async-done(((bf16[512,4096]{1,0:T(8,128)(2,1)}), bf16[128,4096]{1,0:T(8,128)(2,1)}) %reduce-scatter.7.cloned.1.call-update) | async-done | bytes 1048592
  328.5 2.3 fusion.99
  330.7 71.6 %reduce-scatter.5.cloned.1.call-done = bf16[256,4096]{1,0:T(8,128)(2,1)} async-done(((bf16[1024,4096]{1,0:T(8,128)(2,1)}), bf16[256,4096]{1,0:T(8,128)(2,1)}) %reduce-scatter.5.cloned.1.call-update) | async-done | bytes 2097168 | tf_op jit(solution)/shard_map/reduce_scatter | solution.py:173
  402.3 2.7 slice_bitcast_fusion
  406.3 123.6 %all-reduce.2.cloned.1.call-done = f32[2048,8]{0,1:T(8,128)} async-done(((f32[2048,8]{0,1:T(8,128)}), f32[2048,8]{0,1:T(8,128)}) %all-reduce.2.cloned.1.call-update) | async-done | bytes 65552 | tf_op jit(solution)/shard_map/psum | solution.py:144
  530.0 1.5 copy.94
  (116 shorter events, 29.5 us)
Async XLA Ops:
  7.2 52.5 %copy-start = (bf16[128,2048]{1,0:T(8,128)(2,1)S(1)}, bf16[128,2048]{1,0:T(8,128)(2,1)}, u32[]{:S(2)}) copy-start(bf16[128,2048]{1,0:T(8,128)(2,1)} %param.13) | copy-start | bytes 1572868
  7.2 4.2 copy-start.27
  7.2 4.2 copy-start.26
  7.2 27.4 %all-gather.7.cloned.1.call-start = ((), (), s32[]{:S(2)}) async-start(), calls=%async_computation.7 | async-start | bytes 2621440 | tf_op jit(solution)/shard_map/all_gather | solution.py:50
  7.9 51.7 %all-gather.5.cloned.1.call-start = ((), (), s32[]{:S(2)}) async-start(), calls=%async_computation.6 | async-start | bytes 2621440 | tf_op jit(solution)/shard_map/all_gather | solution.py:49
  10.1 94.2 %all-gather.9.cloned.1.call-start = ((), (), s32[]{:S(2)}) async-start(), calls=%async_computation.8 | async-start | bytes 5242880 | tf_op jit(solution)/shard_map/all_gather | solution.py:100
  10.8 121.3 %all-gather.11.cloned.1.call-start = ((), (), s32[]{:S(2)}) async-start(), calls=%async_computation.9 | async-start | bytes 5242880 | tf_op jit(solution)/shard_map/all_gather | solution.py:101
  37.5 25.8 %copy-start.6 = (bf16[512,2048]{0,1:T(8,128)(2,1)}, bf16[512,2048]{0,1:T(8,128)(2,1)S(1)}, u32[]{:S(2)}) copy-start(bf16[512,2048]{0,1:T(8,128)(2,1)S(1)} %copy.54) | copy-start | bytes 6291460
  62.0 2.0 copy-start.1
  67.7 36.6 %copy-start.10 = (bf16[128,2048]{1,0:T(8,128)(2,1)}, bf16[128,2048]{1,0:T(8,128)(2,1)S(1)}, u32[]{:S(2)}) copy-start(bf16[128,2048]{1,0:T(8,128)(2,1)S(1)} %add_convert_fusion.3) | copy-start | bytes 1572868
  110.4 25.9 %copy-start.20 = (bf16[320,1024]{1,0:T(8,128)(2,1)}, bf16[320,1024]{1,0:T(8,128)(2,1)S(1)}, u32[]{:S(2)}) copy-start(bf16[320,1024]{1,0:T(8,128)(2,1)S(1)} %get-tuple-element.54) | copy-start | bytes 1966084
  132.1 3.6 copy-start.13
  137.8 36.3 %copy-start.8 = (bf16[128,2048]{1,0:T(8,128)(2,1)S(1)}, bf16[128,2048]{1,0:T(8,128)(2,1)}, u32[]{:S(2)}) copy-start(bf16[128,2048]{1,0:T(8,128)(2,1)} %param.23) | copy-start | bytes 1572868
  137.9 36.3 %copy-start.23 = (f32[1,2048]{1,0:T(1,128)S(1)}, f32[1,2048]{1,0:T(1,128)}, u32[]{:S(2)}) copy-start(f32[1,2048]{1,0:T(1,128)} %param.18) | copy-start | bytes 24580
  174.1 1.6 copy-start.3
  177.0 34.8 %copy-start.28 = (f32[320,1024]{1,0:T(8,128)S(1)}, f32[320,1024]{1,0:T(8,128)}, u32[]{:S(2)}) copy-start(f32[320,1024]{1,0:T(8,128)} %get-tuple-element.55) | copy-start | bytes 3932164
  211.8 2.2 copy-start.18
  211.8 2.7 copy-start.12
  214.0 2.1 copy-start.22
  218.7 34.3 %all-to-all-start.3 = ((bf16[8,40,2048]{2,1,0:T(8,128)(2,1)}), bf16[8,40,2048]{2,1,0:T(8,128)(2,1)S(1)}, u32[]{:S(2)}, u32[]{:S(2)}) async-start(bf16[8,40,2048]{2,1,0:T(8,128)(2,1)} %bitcast.131), calls=%async_computation.3 | async-start | bytes 2621440 | tf_op jit(solution)/shard_map/all_to_all | solution.py:166
  222.9 105.6 %reduce-scatter.7.cloned.1.call-start = ((), (), s32[]{:S(2)}) async-start(), calls=%async_computation.12 | async-start | bytes 5242880
  254.0 1.2 copy-start.4
  254.1 1.3 copy-start.9
  254.1 1.7 copy-start.14
  257.3 2.5 copy-start.16
  261.2 4.7 copy-start.2
  261.2 4.7 copy-start.7
  284.3 6.2 %copy-start.21 = (bf16[320,1024]{1,0:T(8,128)(2,1)S(1)}, bf16[320,1024]{1,0:T(8,128)(2,1)}, u32[]{:S(2)}) copy-start(bf16[320,1024]{1,0:T(8,128)(2,1)} %copy-done.20) | copy-start | bytes 1966084
  284.3 118.0 %reduce-scatter.5.cloned.1.call-start = ((), (), s32[]{:S(2)}) async-start(), calls=%async_computation.10 | async-start | bytes 10485760 | tf_op jit(solution)/shard_map/reduce_scatter | solution.py:173
  284.4 6.1 %copy-start.19 = (bf16[8,40,2048]{2,1,0:T(8,128)(2,1)S(1)}, bf16[8,40,2048]{2,1,0:T(8,128)(2,1)}, u32[]{:S(2)}) copy-start(bf16[8,40,2048]{2,1,0:T(8,128)(2,1)} %copy-done.18) | copy-start | bytes 3932164
  302.8 1.2 copy-start.11
  302.8 227.1 %all-reduce.2.cloned.1.call-start = ((), (), s32[]{:S(2)}) async-start(), calls=%async_computation.11 | async-start | bytes 131072 | tf_op jit(solution)/shard_map/psum | solution.py:144
  (5 other events, 4.6 us)
Sparse Core Ops, SparseCore 0:
  9.6 25.0 all-gather.6
  36.7 22.8 all-gather.4
  61.2 34.9 all-gather.8
  97.6 34.4 all-gather.10
  284.5 43.9 reduce-scatter.6
  330.9 71.3 reduce-scatter.4
  408.5 121.4 all-reduce.1
where the time goes:
time: 539 us; the launch traced here: 538 us
  waiting for transfers between devices  314 us (58%)
  blocking collectives  106 us (20%)
  matrix products  46.1 us (9%)
  local copies, waits for them, and re-layouts  32.1 us (6%)
  other arithmetic  20.4 us (4%)
  between operations  14.6 us (3%)
    psum x1, waiting for transfers between devices, local(): lax.psum(contract_rows(normed_mod, logit_grad), ('expert', 'ctx'))  124 us
    reduce_scatter x1, waiting for transfers between devices, local(): lax.psum_scatter(jnp.concatenate([contract_rows(pre_grad, rows_flat), con...  71.6 us
    all_to_all x1, blocking collectives, local(): lax.all_to_all(block_sum.astype(jnp.bfloat16).reshape(experts, item_count...  35.8 us
    all_to_all x1, blocking collectives, local(): lax.all_to_all(sent_rows, 'expert', split_axis=0, concat_axis=0, tiled=True)  35.7 us
    all_to_all x1, blocking collectives, local(): lax.all_to_all(sent_grads, 'expert', split_axis=0, concat_axis=0, tiled=T...  34.8 us
    all_to_all x1, waiting for transfers between devices, local(): lax.all_to_all(block_sum.astype(jnp.bfloat16).reshape(experts, capacity,...  29.9 us
    all_gather x1, waiting for transfers between devices, local(): lax.all_gather(values, 'ctx', axis=0, tiled=True)  22.9 us
    unnamed x8, waiting for transfers between devices  22.3 us
  transfers between devices with their start and end apart: 8, of which 7 were waited for; matrix products, arithmetic and copies ran while one was open for 9% of the time, Pallas kernels for 0%

commit v1 on v0

--- a/solution.py
+++ b/solution.py
@@ -141,7 +141,9 @@
         * gate_two
     )
     logit_grad = (gate_tilt[:, None] * (first_hot - second_hot)).astype(jnp.bfloat16)
-    grad_router = lax.psum(contract_rows(normed_mod, logit_grad), ("expert", "ctx"))
+    grad_router = jnp.sum(
+        lax.all_gather(contract_rows(normed_mod, logit_grad), ("expert", "ctx")), axis=0
+    )
     back_router = contract_cols(logit_grad, router)
     sent_grads = (contract_rows(pick_one, grad_one) + contract_rows(pick_two, grad_two)).astype(
         jnp.bfloat16

time: 539 us -> 423 us (0.78)
  waiting for transfers between devices: 314 us -> 196 us
    psum x1 -> x0, waiting for transfers between devices: 124 us -> none  [local(): lax.psum(contract_rows(normed_mod, logit_grad), ('expert', 'ctx'))]
    unnamed x8, waiting for transfers between devices: 22.3 us -> 28.9 us
    unnamed x65 -> x60, local copies, waits for them, and re-layouts: 19.4 us -> 16.6 us
  transfers between devices with their start and end apart: 8 -> 8, of which waited for: 7 -> 6; matrix products, arithmetic and copies ran while one was open for 9% -> 18% of each run, Pallas kernels for 0% -> 0%
where the time goes in v1:
time: 423 us; the launch traced here: 421 us
  waiting for transfers between devices  196 us (46%)
  blocking collectives  106 us (25%)
  matrix products  48.6 us (11%)
  local copies, waits for them, and re-layouts  29.3 us (7%)
  other arithmetic  21.3 us (5%)
  between operations  14.6 us (3%)
  starting transfers between devices  4.91 us (1%)
    reduce_scatter x1, waiting for transfers between devices, local(): lax.psum_scatter(jnp.concatenate([contract_rows(pre_grad, rows_flat), con...  71.8 us
    all_to_all x1, blocking collectives, local(): lax.all_to_all(block_sum.astype(jnp.bfloat16).reshape(experts, item_count...  35.8 us
    all_to_all x1, blocking collectives, local(): lax.all_to_all(sent_rows, 'expert', split_axis=0, concat_axis=0, tiled=True)  35.7 us
    all_to_all x1, blocking collectives, local(): lax.all_to_all(sent_grads, 'expert', split_axis=0, concat_axis=0, tiled=T...  34.8 us
    all_to_all x1, waiting for transfers between devices, local(): lax.all_to_all(block_sum.astype(jnp.bfloat16).reshape(experts, capacity,...  29.4 us
    unnamed x8, waiting for transfers between devices  28.9 us
    all_gather x1, waiting for transfers between devices, local(): lax.all_gather(values, 'ctx', axis=0, tiled=True)  22.9 us
    all_gather x1, waiting for transfers between devices, local(): lax.all_gather(keys, 'ctx', axis=0, tiled=True)  22.1 us
  transfers between devices with their start and end apart: 8, of which 6 were waited for; matrix products, arithmetic and copies ran while one was open for 18% of the time, Pallas kernels for 0%

profile of v1, /device:TPU:1, one launch (start us, length us, event | category | flops | bytes accessed | tf_op | source)
XLA Modules:
  0.0 421.1 jit_solution(6660232893982055955)
XLA Ops:
  8.0 2.0 copy.51
  11.7 22.9 %all-gather.9.cloned.1.call-done = bf16[512,2048]{1,0:T(8,128)(2,1)} async-done(((bf16[128,2048]{1,0:T(8,128)(2,1)}), bf16[512,2048]{1,0:T(8,128)(2,1)}) %all-gather.9.cloned.1.call-update) | async-done | bytes 2097168 | tf_op jit(solution)/shard_map/all_gather | solution.py:50
  34.6 2.9 copy.54
  37.5 22.1 %all-gather.7.cloned.1.call-done = bf16[512,2048]{0,1:T(8,128)(2,1)} async-done(((bf16[128,2048]{0,1:T(8,128)(2,1)}), bf16[512,2048]{0,1:T(8,128)(2,1)}) %all-gather.7.cloned.1.call-update) | async-done | bytes 2097168 | tf_op jit(solution)/shard_map/all_gather | solution.py:49
  59.6 2.4 multiply_reduce_fusion
  69.0 35.7 %all_to_all.20 = bf16[8,40,2048]{2,1,0:T(8,128)(2,1)S(1)} all-to-all(bf16[8,40,2048]{2,1,0:T(8,128)(2,1)S(1)} %bitcast.131), channel_id=1, replica_groups=mesh['expert'=8,'ctx'=4] {'expert'}, dimensions={0} | all-to-all | bytes 2621440 | tf_op jit(solution)/shard_map/all_to_all | solution.py:105
  104.7 6.3 %multiply_convert_fusion.2 = (bf16[320,1024]{1,0:T(8,128)(2,1)}, f32[320,1024]{1,0:T(8,128)}) fusion(bf16[320,2048]{1,0:T(8,128)(2,1)S(1)} %bitcast.142, bf16[1,2048,1024]{2,1,0:T(8,128)(2,1)} %all-gather.11.cloned.1.call-done), kind=kOutput, calls=%fused_computation.55 | convolution fusion | flops 1345126400 | bytes 7471104 | tf_op jit(solution)/shard_map/dot_general | solution.py:108
  111.0 21.1 %all-gather.13.cloned.1.call-done = bf16[1,1024,2048]{2,1,0:T(8,128)(2,1)} async-done(((bf16[1,256,2048]{2,1,0:T(8,128)(2,1)}), bf16[1,1024,2048]{2,1,0:T(8,128)(2,1)}) %all-gather.13.cloned.1.call-update) | async-done | bytes 4194320 | tf_op jit(solution)/shard_map/all_gather | solution.py:101
  132.1 2.0 convolution_convert_fusion.7
  134.1 1.7 convolution_convert_fusion.8
  137.9 35.8 %all_to_all.21 = bf16[8,40,2048]{2,1,0:T(8,128)(2,1)S(1)} all-to-all(bf16[8,40,2048]{2,1,0:T(8,128)(2,1)S(1)} %bitcast.133), channel_id=1, replica_groups=mesh['expert'=8,'ctx'=4] {'expert'}, dimensions={0} | all-to-all | bytes 2621440 | tf_op jit(solution)/shard_map/all_to_all | solution.py:120
  177.1 34.8 %all_to_all.22 = bf16[8,40,2048]{2,1,0:T(8,128)(2,1)S(1)} all-to-all(bf16[8,40,2048]{2,1,0:T(8,128)(2,1)S(1)} %bitcast.130), channel_id=1, replica_groups=mesh['expert'=8,'ctx'=4] {'expert'}, dimensions={0} | all-to-all | bytes 2621440 | tf_op jit(solution)/shard_map/all_to_all | solution.py:152
  211.9 2.2 fusion.31
  216.8 2.0 add_convert_fusion
  218.8 4.1 all-to-all-start.3
  223.0 1.9 fusion.84
  225.2 29.4 %all-to-all-done.3 = bf16[8,40,2048]{2,1,0:T(8,128)(2,1)S(1)} async-done(((bf16[8,40,2048]{2,1,0:T(8,128)(2,1)}), bf16[8,40,2048]{2,1,0:T(8,128)(2,1)S(1)}, u32[]{:S(2)}, u32[]{:S(2)}) %all-to-all-start.3) | async-done | bytes 1310752 | tf_op jit(solution)/shard_map/all_to_all | solution.py:168
  261.6 4.2 multiply_convert_fusion.1
  265.8 2.2 fusion.17
  268.0 3.9 copy.62
  272.0 3.3 convert_bitcast_fusion
  275.3 2.2 pad_maximum_fusion.1
  277.5 6.4 %copy.77 = bf16[512,4096]{1,0:T(8,128)(2,1)} copy(bf16[512,4096]{0,1:T(8,128)(2,1)} %pad_maximum_fusion.1) | data formatting | bytes 8388608
  284.3 5.9 %convolution_convert_fusion.1 = bf16[1024,2048]{1,0:T(8,128)(2,1)} fusion(bf16[320,1024]{1,0:T(8,128)(2,1)} %copy-done.20, bf16[320,2048]{1,0:T(8,128)(2,1)} %bitcast.143), kind=kOutput, calls=%fused_computation.9 | convolution fusion | flops 1344274432 | bytes 6160384 | tf_op jit(solution)/shard_map/dot_general | solution.py:16
  290.3 4.4 %convolution_convert_fusion = bf16[1024,2048]{1,0:T(8,128)(2,1)} fusion(bf16[320,1024]{1,0:T(8,128)(2,1)S(1)} %copy-done.19, bf16[320,2048]{1,0:T(8,128)(2,1)S(1)} %bitcast.145), kind=kOutput, calls=%fused_computation.8 | convolution fusion | flops 1344274432 | bytes 6160384 | tf_op jit(solution)/shard_map/dot_general | solution.py:16
  294.6 9.0 %pad_maximum_fusion = bf16[1024,4096]{1,0:T(8,128)(2,1)} fusion(bf16[1024,2048]{1,0:T(8,128)(2,1)} %convolution_convert_fusion, bf16[1024,2048]{1,0:T(8,128)(2,1)} %convolution_convert_fusion.1), kind=kLoop, calls=%fused_computation | loop fusion | flops 16777216 | bytes 16777216 | tf_op jit(solution)/shard_map/concatenate | solution.py:176
  303.7 2.3 reduce_sum.99
  306.0 2.3 fusion.32
  309.3 26.9 %reduce-scatter.7.cloned.1.call-done = bf16[128,4096]{1,0:T(8,128)(2,1)} async-done(((bf16[512,4096]{1,0:T(8,128)(2,1)}), bf16[128,4096]{1,0:T(8,128)(2,1)}) %reduce-scatter.7.cloned.1.call-update) | async-done | bytes 1048592
  336.2 2.3 fusion.99
  338.5 71.8 %reduce-scatter.5.cloned.1.call-done = bf16[256,4096]{1,0:T(8,128)(2,1)} async-done(((bf16[1024,4096]{1,0:T(8,128)(2,1)}), bf16[256,4096]{1,0:T(8,128)(2,1)}) %reduce-scatter.5.cloned.1.call-update) | async-done | bytes 2097168 | tf_op jit(solution)/shard_map/reduce_scatter | solution.py:175
  410.3 2.7 slice_bitcast_fusion
  (112 shorter events, 27.4 us)
Async XLA Ops:
  7.2 52.5 %copy-start = (bf16[128,2048]{1,0:T(8,128)(2,1)S(1)}, bf16[128,2048]{1,0:T(8,128)(2,1)}, u32[]{:S(2)}) copy-start(bf16[128,2048]{1,0:T(8,128)(2,1)} %param.13) | copy-start | bytes 1572868
  7.2 4.2 copy-start.25
  7.2 4.2 copy-start.24
  7.2 27.4 %all-gather.9.cloned.1.call-start = ((), (), s32[]{:S(2)}) async-start(), calls=%async_computation.7 | async-start | bytes 2621440 | tf_op jit(solution)/shard_map/all_gather | solution.py:50
  7.9 51.7 %all-gather.7.cloned.1.call-start = ((), (), s32[]{:S(2)}) async-start(), calls=%async_computation.6 | async-start | bytes 2621440 | tf_op jit(solution)/shard_map/all_gather | solution.py:49
  10.0 94.7 %all-gather.11.cloned.1.call-start = ((), (), s32[]{:S(2)}) async-start(), calls=%async_computation.8 | async-start | bytes 5242880 | tf_op jit(solution)/shard_map/all_gather | solution.py:100
  10.8 121.3 %all-gather.13.cloned.1.call-start = ((), (), s32[]{:S(2)}) async-start(), calls=%async_computation.9 | async-start | bytes 5242880 | tf_op jit(solution)/shard_map/all_gather | solution.py:101
  37.5 25.8 %copy-start.5 = (bf16[512,2048]{0,1:T(8,128)(2,1)}, bf16[512,2048]{0,1:T(8,128)(2,1)S(1)}, u32[]{:S(2)}) copy-start(bf16[512,2048]{0,1:T(8,128)(2,1)S(1)} %copy.54) | copy-start | bytes 6291460
  62.0 2.0 copy-start.1
  65.0 0.8 copy-start.13
  65.8 1.0 copy-start.4
  65.9 1.2 copy-start.23
  104.7 6.3 %copy-start.15 = (bf16[8,40,2048]{2,1,0:T(8,128)(2,1)}, bf16[8,40,2048]{2,1,0:T(8,128)(2,1)S(1)}, u32[]{:S(2)}) copy-start(bf16[8,40,2048]{2,1,0:T(8,128)(2,1)S(1)} %all_to_all.20) | copy-start | bytes 3932164
  132.1 2.0 copy-start.18
  132.1 3.7 copy-start.11
  137.9 36.3 %copy-start.6 = (bf16[128,2048]{1,0:T(8,128)(2,1)S(1)}, bf16[128,2048]{1,0:T(8,128)(2,1)}, u32[]{:S(2)}) copy-start(bf16[128,2048]{1,0:T(8,128)(2,1)} %param.23) | copy-start | bytes 1572868
  137.9 36.3 %copy-start.21 = (f32[1,2048]{1,0:T(1,128)S(1)}, f32[1,2048]{1,0:T(1,128)}, u32[]{:S(2)}) copy-start(f32[1,2048]{1,0:T(1,128)} %param.18) | copy-start | bytes 24580
  174.2 1.6 copy-start.2
  177.1 34.8 %copy-start.26 = (f32[320,1024]{1,0:T(8,128)S(1)}, f32[320,1024]{1,0:T(8,128)}, u32[]{:S(2)}) copy-start(f32[320,1024]{1,0:T(8,128)} %get-tuple-element.55) | copy-start | bytes 3932164
  211.9 2.2 copy-start.16
  211.9 2.7 copy-start.10
  214.1 2.1 copy-start.20
  218.8 35.8 %all-to-all-start.3 = ((bf16[8,40,2048]{2,1,0:T(8,128)(2,1)}), bf16[8,40,2048]{2,1,0:T(8,128)(2,1)S(1)}, u32[]{:S(2)}, u32[]{:S(2)}) async-start(bf16[8,40,2048]{2,1,0:T(8,128)(2,1)} %bitcast.132), calls=%async_computation.3 | async-start | bytes 2621440 | tf_op jit(solution)/shard_map/all_to_all | solution.py:168
  222.9 80.7 %all-gather.15.cloned.1.call-start = ((), (), s32[]{:S(2)}) async-start(), calls=%async_computation.11 | async-start | bytes 2162688 | tf_op jit(solution)/shard_map/all_gather | solution.py:145
  224.9 111.4 %reduce-scatter.7.cloned.1.call-start = ((), (), s32[]{:S(2)}) async-start(), calls=%async_computation.12 | async-start | bytes 5242880
  255.5 1.2 copy-start.3
  255.5 1.3 copy-start.7
  255.6 1.7 copy-start.12
  272.0 3.3 copy-start.9
  284.0 6.3 %copy-start.19 = (bf16[320,1024]{1,0:T(8,128)(2,1)S(1)}, bf16[320,1024]{1,0:T(8,128)(2,1)}, u32[]{:S(2)}) copy-start(bf16[320,1024]{1,0:T(8,128)(2,1)} %get-tuple-element.54) | copy-start | bytes 1966084
  284.0 126.3 %reduce-scatter.5.cloned.1.call-start = ((), (), s32[]{:S(2)}) async-start(), calls=%async_computation.10 | async-start | bytes 10485760 | tf_op jit(solution)/shard_map/reduce_scatter | solution.py:175
  284.3 6.0 %copy-start.17 = (bf16[8,40,2048]{2,1,0:T(8,128)(2,1)S(1)}, bf16[8,40,2048]{2,1,0:T(8,128)(2,1)}, u32[]{:S(2)}) copy-start(bf16[8,40,2048]{2,1,0:T(8,128)(2,1)} %copy-done.16) | copy-start | bytes 3932164
  (3 other events, 2.3 us)
Sparse Core Ops, SparseCore 0:
  9.6 25.0 all-gather.8
  36.7 22.8 all-gather.6
  61.2 34.9 all-gather.10
  97.6 34.4 all-gather.12
  226.9 64.0 all-gather.14
  293.3 42.8 reduce-scatter.6
  338.8 71.4 reduce-scatter.4
